TPU v7x, 32 devices: a whole 2x2x4 slice. The times are simulated.
32 devices in a mesh: row: 4 (over z), col: 8 (over y, x, core).
Axes of the slice: x: 2, y: 2, z: 4, core: 2. Of those that a mesh axis runs over, the one named last changes fastest.
Arguments:
- resistance: float32 [768, 1024], P('row', 'col'), may hold values from 1 to 100
- ground: float32 [768, 1024], P('row', 'col'), may hold values from 0.001 to 0.01
- nodata: int32 [768, 1024], P('row', 'col'), may hold values 0 or 1
- patch_ids: int32 [768, 1024], P('row', 'col'), may hold values from 0 to 8
Outputs:
- correction: float32 [8, 768, 1024], P(None, 'row', 'col')
All inputs are finite; a program needn't handle non-finite values. No bound on the sum of `nodata` on one device may be relied on, other than what follows from the above.
Results may differ from a plain program's by a relative error of at most 0.0003.
Values sent between devices are 32-bit elements; how exact they have to be, the bound alone decides.
No kernel may reach another device: no remote copies, remote signals or barrier semaphores. Data moves between devices by JAX's collectives and lax.ppermute only.
A program may use at most 128 MiB of HBM per device.

v0:
```python
from functools import partial
import jax
import jax.numpy as jnp
from jax import lax
from jax.sharding import PartitionSpec as P

RHS = 8
ITERS = 4
OMEGA = 0.8


def padded_2(block, sides, width):
    for axis, dim in sides:
        count = lax.axis_size(axis)
        forward = [(i, i + 1) for i in range(count - 1)]
        backward = [(target, source) for source, target in forward]
        low = lax.ppermute(
            lax.slice_in_dim(block, block.shape[dim] - width, None, axis=dim), axis, forward
        )
        high = lax.ppermute(lax.slice_in_dim(block, 0, width, axis=dim), axis, backward)
        block = jnp.concatenate([low, block, high], axis=dim)
    return block


def shifted(block, axis, distance):
    devices = range(lax.axis_size(axis))
    route = [(i - distance, i) for i in devices if i - distance in devices]
    return lax.ppermute(block, axis, route)


def partner_2(shard, axis, apart):
    return lax.ppermute(shard, axis, [(i, i ^ 1 << apart) for i in range(lax.axis_size(axis))])


def conductance(resist, validity, near_resist, near_valid):
    return validity * near_valid * (2.0 / (resist + near_resist))


def edge_terms(res_pad, val_pad):
    resist = res_pad[1:-1, 1:-1]
    validity = val_pad[1:-1, 1:-1]
    north_link = conductance(resist, validity, res_pad[:-2, 1:-1], val_pad[:-2, 1:-1])
    south_link = conductance(resist, validity, res_pad[2:, 1:-1], val_pad[2:, 1:-1])
    west_link = conductance(resist, validity, res_pad[1:-1, :-2], val_pad[1:-1, :-2])
    east_link = conductance(resist, validity, res_pad[1:-1, 2:], val_pad[1:-1, 2:])
    return (north_link, south_link, west_link, east_link)


def diagonal_of(coeffs):
    return coeffs[0] + coeffs[1] + coeffs[2] + coeffs[3] + coeffs[4]


def apply_operator(values, coeffs, sides):
    above_cells, below_cells, left_cells, right_cells = sides
    pulled = (
        coeffs[1] * above_cells
        + coeffs[2] * below_cells
        + coeffs[3] * left_cells
        + coeffs[4] * right_cells
    )
    return diagonal_of(coeffs) * values - pulled


def restrict_field(values):
    count, rows_here, cols_here = values.shape
    return values.reshape(count, rows_here // 2, 2, cols_here // 2, 2).sum(axis=(2, 4))


def coarse_coeffs(coeffs):
    count, rows_here, cols_here = coeffs.shape
    blocks = coeffs.reshape(count, rows_here // 2, 2, cols_here // 2, 2)
    leakage = blocks[0].sum(axis=(1, 3))
    north_link = blocks[1][:, 0].sum(axis=-1)
    south_link = blocks[2][:, 1].sum(axis=-1)
    west_link = blocks[3][:, :, :, 0].sum(axis=1)
    east_link = blocks[4][:, :, :, 1].sum(axis=1)
    return jnp.stack([leakage, north_link, south_link, west_link, east_link])


def prolong(values):
    return jnp.repeat(jnp.repeat(values, 2, axis=1), 2, axis=2)


def halo_sides(values):
    padded = padded_2(values, (("row", 1), ("col", 2)), 1)
    return (padded[:, :-2, 1:-1], padded[:, 2:, 1:-1], padded[:, 1:-1, :-2], padded[:, 1:-1, 2:])


def rim_sides(values, distance):
    above_rim = shifted(values[:, -1:, :], "row", distance)
    below_rim = shifted(values[:, :1, :], "row", -distance)
    left_rim = shifted(values[:, :, -1:], "col", distance)
    right_rim = shifted(values[:, :, :1], "col", -distance)
    above_cells = jnp.concatenate([above_rim, values[:, :-1, :]], axis=1)
    below_cells = jnp.concatenate([values[:, 1:, :], below_rim], axis=1)
    left_cells = jnp.concatenate([left_rim, values[:, :, :-1]], axis=2)
    right_cells = jnp.concatenate([values[:, :, 1:], right_rim], axis=2)
    return (above_cells, below_cells, left_cells, right_cells)


def descend(residual, coeffs, sides_of):
    smoothed = OMEGA * residual / diagonal_of(coeffs)
    remainder = residual - apply_operator(smoothed, coeffs, sides_of(smoothed))
    return (smoothed, restrict_field(remainder), coarse_coeffs(coeffs))


def merge_tiles(payload, bit_index):
    partner = partner_2(payload, "row", bit_index)
    is_first = (lax.axis_index("row") >> bit_index) % 2 == 0
    payload = jnp.where(
        is_first,
        jnp.concatenate([payload, partner], axis=1),
        jnp.concatenate([partner, payload], axis=1),
    )
    partner = partner_2(payload, "col", bit_index)
    is_first = (lax.axis_index("col") >> bit_index) % 2 == 0
    return jnp.where(
        is_first,
        jnp.concatenate([payload, partner], axis=2),
        jnp.concatenate([partner, payload], axis=2),
    )


def merge_level(residual, coeffs, bit_index):
    sources = residual.shape[0]
    merged = merge_tiles(jnp.concatenate([residual, coeffs], axis=0), bit_index)
    return (merged[:sources], merged[sources:])


def own_part(whole_grid, shift_bits, pieces, rows_here, cols_here):
    row_at = (lax.axis_index("row") >> shift_bits) % pieces
    col_at = (lax.axis_index("col") >> shift_bits) % pieces
    starts = (jnp.int32(0), row_at * rows_here, col_at * cols_here)
    return lax.dynamic_slice(whole_grid, starts, (whole_grid.shape[0], rows_here, cols_here))


def coarse_solve(rhs_grid, coeffs):
    sides_of = partial(rim_sides, distance=4)
    owner_weight = jnp.logical_and(
        lax.axis_index("row") % 4 == 0, lax.axis_index("col") % 4 == 0
    ).astype(jnp.float32)

    def local_dot(first, second):
        return owner_weight * jnp.sum(first * second, axis=(1, 2))

    def norm_sum(values):
        return lax.psum(local_dot(values, values), ("row", "col"))

    def expand(scalars):
        return scalars[:, None, None]

    solution = jnp.zeros_like(rhs_grid)
    residual = rhs_grid
    direction = residual
    norm_now = norm_sum(residual)
    for sweep in range(ITERS):
        image = apply_operator(direction, coeffs, sides_of(direction))
        step_size = norm_now / lax.psum(local_dot(direction, image), ("row", "col"))
        solution = solution + expand(step_size) * direction
        if sweep + 1 < ITERS:
            residual = residual - expand(step_size) * image
            norm_next = norm_sum(residual)
            direction = residual + expand(norm_next / norm_now) * direction
            norm_now = norm_next
    return solution


def shards(resistance, ground, nodata, patch_ids):
    validity = (nodata == 0).astype(jnp.float32)
    padded = padded_2(jnp.stack([resistance, validity]), (("row", 1), ("col", 2)), 1)
    coeffs = jnp.stack([ground] + list(edge_terms(padded[0], padded[1])))
    sources = jnp.arange(RHS, dtype=jnp.int32)[:, None, None]
    residual = validity[None] * (
        (patch_ids[None] == sources + 1).astype(jnp.float32)
        - 0.125 * (patch_ids[None] > 0).astype(jnp.float32)
    )
    smooth_a, residual, coeffs_b = descend(residual, coeffs, halo_sides)
    smooth_b, residual, coeffs_c = descend(residual, coeffs_b, halo_sides)
    smooth_c, residual, coeffs_d = descend(residual, coeffs_c, halo_sides)
    rows_d = residual.shape[1]
    cols_d = residual.shape[2]
    residual, coeffs_d = merge_level(residual, coeffs_d, 0)
    smooth_d, residual, coeffs_e = descend(residual, coeffs_d, partial(rim_sides, distance=2))
    residual, coeffs_e = merge_level(residual, coeffs_e, 1)
    solution = coarse_solve(residual, coeffs_e)
    upward = smooth_d + own_part(prolong(solution), 1, 2, 2 * rows_d, 2 * cols_d)
    upward = own_part(prolong(upward), 0, 2, 2 * rows_d, 2 * cols_d)
    upward = smooth_c + upward
    upward = smooth_b + prolong(upward)
    return smooth_a + prolong(upward)


def solution(mesh):
    in_specs = (P("row", "col"), P("row", "col"), P("row", "col"), P("row", "col"))
    out_specs = P(None, "row", "col")
    return jax.shard_map(shards, mesh=mesh, in_specs=in_specs, out_specs=out_specs, check_vma=False)
```

profile of v0, /device:TPU:0, one launch (start us, length us, event | category | flops | bytes accessed | tf_op | source)
XLA Modules:
  0.0 562.9 jit_solution(4791267187569328202)
XLA Ops:
  1.6 4.9 collective-permute-start
  8.8 3.2 collective-permute-done.1
  17.3 8.4 %squeeze.46 = f32[96,2,64,2]{3,2,1,0:T(8,128)} reshape(f32[192,128]{1,0:T(8,128)} %param.5) | data formatting | bytes 196608 | tf_op jit(solution)/shard_map/squeeze | solution.py:72
  25.6 3.7 reduce_sum.289
  34.1 7.6 %squeeze.47 = f32[96,2,64,2]{3,2,1,0:T(8,128)} reshape(f32[192,128]{1,0:T(8,128)S(1)} %get-tuple-element.19) | data formatting | bytes 196608 | tf_op jit(solution)/shard_map/squeeze | solution.py:73
  41.6 7.6 %squeeze.48 = f32[96,2,64,2]{3,2,1,0:T(8,128)} reshape(f32[192,128]{1,0:T(8,128)S(1)} %get-tuple-element.20) | data formatting | bytes 196608 | tf_op jit(solution)/shard_map/squeeze | solution.py:74
  49.2 4.6 slice_reduce_fusion.2
  54.0 7.6 %squeeze.49 = f32[96,2,64,2]{3,2,1,0:T(8,128)} reshape(f32[192,128]{1,0:T(8,128)S(1)} %get-tuple-element.21) | data formatting | bytes 196608 | tf_op jit(solution)/shard_map/squeeze | solution.py:75
  61.6 7.8 %squeeze.50 = f32[96,2,64,2]{3,2,1,0:T(8,128)} reshape(f32[192,128]{1,0:T(8,128)S(1)} %get-tuple-element.22) | data formatting | bytes 196608 | tf_op jit(solution)/shard_map/squeeze | solution.py:76
  69.4 7.9 %slice_reduce_fusion = (f32[96,64]{1,0:T(8,128)S(1)}, f32[96,64]{1,0:T(8,128)S(1)}) fusion(f32[96,2,64,2]{3,2,1,0:T(8,128)} %squeeze.50, f32[96,2,64,2]{3,2,1,0:T(8,128)} %squeeze.49), kind=kLoop, calls=%fused_computation | loop fusion | flops 12288 | bytes 147456 | tf_op jit(solution)/shard_map/reduce_sum | solution.py:76
  86.7 3.5 collective-permute-start.4
  91.8 8.8 %collective-permute-done.4 = f32[8,1,128]{1,0,2:T(8,128)S(1)} collective-permute-done((f32[8,1,128]{1,0,2:T(8,128)S(1)}, f32[8,1,128]{1,0,2:T(8,128)S(1)}, u32[]{:S(2)}, u32[]{:S(2)}) %collective-permute-start.4) | collective-permute-done | bytes 4128 | tf_op jit(solution)/shard_map/ppermute | solution.py:17
  100.6 4.7 collective-permute-done.5
  106.1 3.3 collective-permute-start.6
  115.4 4.1 fusion.3
  119.5 7.0 %copy.453 = f32[8,192,128]{0,2,1:T(8,128)} copy(f32[8,192,128]{1,0,2:T(8,128)S(1)} %fusion.3) | data formatting | bytes 1572864 | tf_op jit(solution)/shard_map/sub | solution.py:103
  126.5 14.0 %reduce_sum.288 = f32[8,96,64]{0,2,1:T(8,128)S(1)} reduce(f32[8,96,2,64,2]{0,4,3,2,1:T(2,128)} %bitcast.80, f32[]{:T(128)} %constant.67.clone.1), dimensions={2,4}, to_apply=%region_0.0 | reduce | flops 147456 | bytes 983044 | tf_op jit(solution)/shard_map/reduce_sum | solution.py:66
  143.4 3.5 collective-permute-start.8
  150.9 4.7 collective-permute-done.9
  155.7 4.1 collective-permute-start.10
  162.9 3.6 collective-permute-done.11
  167.8 3.7 copy.461
  171.5 3.9 reduce_sum.294
  177.9 2.2 collective-permute-start.12
  183.4 3.9 collective-permute-done.13
  187.4 2.8 collective-permute-start.14
  193.1 2.5 collective-permute-done.15
  198.2 5.9 %collective-permute-done.16 = f32[13,24,16]{0,2,1:T(8,128)S(1)} collective-permute-done((f32[13,24,16]{0,2,1:T(8,128)S(1)}, f32[13,24,16]{0,2,1:T(8,128)S(1)}, u32[]{:S(2)}, u32[]{:S(2)}) %collective-permute-start.16) | collective-permute-done | bytes 20000 | tf_op jit(solution)/shard_map/ppermute | solution.py:32
  209.7 4.5 collective-permute-start.20
  221.6 3.6 collective-permute-start.22
  225.4 7.4 %collective-permute-done.22 = f32[13,24,16]{0,2,1:T(8,128)S(1)} collective-permute-done((f32[13,24,16]{0,2,1:T(8,128)S(1)}, f32[13,24,16]{0,2,1:T(8,128)S(1)}, u32[]{:S(2)}, u32[]{:S(2)}) %collective-permute-start.22) | collective-permute-done | bytes 20000 | tf_op jit(solution)/shard_map/ppermute | solution.py:32
  233.1 2.3 collective-permute-start.23
  235.4 3.2 collective-permute-done.23
  240.1 3.4 collective-permute-start.26
  244.9 4.2 collective-permute-done.27
  249.3 37.8 %all-reduce = (f32[8]{0:T(128)S(1)}, f32[8]{0:T(128)S(1)}) all-reduce(f32[8]{0:T(128)S(1)} %broadcast_multiply_fusion.7, f32[8]{0:T(128)S(1)} %broadcast_multiply_fusion.6), channel_id=1, replica_groups=mesh['row'=4,'col'=8] {'row','col'}, use_global_device_ids=true, to_apply=%region_25.26 | all-reduce | flops 16 | bytes 128 | tf_op jit(solution)/shard_map/psum | solution.py:147
  287.3 40.3 %psum.58 = f32[8]{0:T(128)S(1)} all-reduce(f32[8]{0:T(128)S(1)} %broadcast_multiply_fusion.5), channel_id=1, replica_groups=mesh['row'=4,'col'=8] {'row','col'}, use_global_device_ids=true, to_apply=%region_29.30 | all-reduce | flops 8 | bytes 64 | tf_op jit(solution)/shard_map/psum | solution.py:147
  329.2 4.2 collective-permute-start.30
  334.7 4.1 collective-permute-done.31
  339.1 37.6 %psum.59 = f32[8]{0:T(128)S(1)} all-reduce(f32[8]{0:T(128)S(1)} %broadcast_multiply_fusion.4), channel_id=1, replica_groups=mesh['row'=4,'col'=8] {'row','col'}, use_global_device_ids=true, to_apply=%region_31.32 | all-reduce | flops 8 | bytes 64 | tf_op jit(solution)/shard_map/psum | solution.py:158
  377.0 41.9 %psum.60 = f32[8]{0:T(128)S(1)} all-reduce(f32[8]{0:T(128)S(1)} %broadcast_multiply_fusion.3), channel_id=1, replica_groups=mesh['row'=4,'col'=8] {'row','col'}, use_global_device_ids=true, to_apply=%region_33.34 | all-reduce | flops 8 | bytes 64 | tf_op jit(solution)/shard_map/psum | solution.py:147
  420.5 4.2 collective-permute-start.34
  426.1 4.1 collective-permute-done.35
  430.5 37.6 %psum.61 = f32[8]{0:T(128)S(1)} all-reduce(f32[8]{0:T(128)S(1)} %broadcast_multiply_fusion.2), channel_id=1, replica_groups=mesh['row'=4,'col'=8] {'row','col'}, use_global_device_ids=true, to_apply=%region_35.36 | all-reduce | flops 8 | bytes 64 | tf_op jit(solution)/shard_map/psum | solution.py:158
  468.3 40.5 %psum.62 = f32[8]{0:T(128)S(1)} all-reduce(f32[8]{0:T(128)S(1)} %broadcast_multiply_fusion.1), channel_id=1, replica_groups=mesh['row'=4,'col'=8] {'row','col'}, use_global_device_ids=true, to_apply=%region_37.38 | all-reduce | flops 8 | bytes 64 | tf_op jit(solution)/shard_map/psum | solution.py:147
  510.4 4.2 collective-permute-start.38
  516.0 4.1 collective-permute-done.39
  520.3 37.9 %psum.63 = f32[8]{0:T(128)S(1)} all-reduce(f32[8]{0:T(128)S(1)} %broadcast_multiply_fusion), channel_id=1, replica_groups=mesh['row'=4,'col'=8] {'row','col'}, use_global_device_ids=true, to_apply=%region_39.40 | all-reduce | flops 8 | bytes 64 | tf_op jit(solution)/shard_map/psum | solution.py:158
  (282 shorter events, 84.4 us)
Async XLA Ops:
  1.6 7.2 %collective-permute-start = (f32[2,1,128]{2,1,0:T(1,128)S(1)}, f32[2,1,128]{2,1,0:T(1,128)S(1)}, u32[]{:S(2)}, u32[]{:S(2)}) collective-permute-start(f32[2,1,128]{2,1,0:T(1,128)S(1)} %get-tuple-element.60), channel_id=1, source_target_pairs={{0,8},{8,16},{16,24},{1,9},{9,17},{17,25},{2,10},{10,18},{18,26},{... | collective-permute-start | bytes 3080 | tf_op jit(solution)/shard_map/ppermute | solution.py:17
  6.6 5.5 collective-permute-start.1
  13.1 18.8 %collective-permute-start.2 = (f32[2,194,1]{2,1,0:T(8,128)S(1)}, f32[2,194,1]{2,1,0:T(8,128)S(1)}, u32[]{:S(2)}, u32[]{:S(2)}) collective-permute-start(f32[2,194,1]{2,1,0:T(8,128)S(1)} %get-tuple-element.58), channel_id=1, source_target_pairs={{0,1},{1,2},{2,3},{3,4},{4,5},{5,6},{6,7},{8,9},{9,10},{10,11},{11... | collective-permute-start | bytes 4664 | tf_op jit(solution)/shard_map/ppermute | solution.py:17
  14.4 17.5 %collective-permute-start.3 = (f32[2,194,1]{2,1,0:T(8,128)S(1)}, f32[2,194,1]{2,1,0:T(8,128)}, u32[]{:S(2)}, u32[]{:S(2)}) collective-permute-start(f32[2,194,1]{2,1,0:T(8,128)S(1)} %get-tuple-element.59), channel_id=1, source_target_pairs={{1,0},{2,1},{3,2},{4,3},{5,4},{6,5},{7,6},{9,8},{10,9},{11,10},{12... | collective-permute-start | bytes 4664 | tf_op jit(solution)/shard_map/ppermute | solution.py:20
  30.6 84.8 %copy-start = (f32[192,128]{0,1:T(8,128)}, f32[192,128]{0,1:T(8,128)S(1)}, u32[]{:S(2)}) copy-start(f32[192,128]{0,1:T(8,128)S(1)} %copy.445) | copy-start | bytes 294916
  30.7 84.7 %copy-start.2 = (f32[192,128]{0,1:T(8,128)}, f32[192,128]{0,1:T(8,128)S(1)}, u32[]{:S(2)}) copy-start(f32[192,128]{0,1:T(8,128)S(1)} %copy.447) | copy-start | bytes 294916
  53.9 24.8 %copy-start.13 = (f32[96,64]{0,1:T(8,128)}, f32[96,64]{0,1:T(8,128)S(1)}, u32[]{:S(2)}) copy-start(f32[96,64]{0,1:T(8,128)S(1)} %copy.457) | copy-start | bytes 73732
  54.0 26.3 %copy-start.15 = (f32[96,64]{0,1:T(8,128)}, f32[96,64]{0,1:T(8,128)S(1)}, u32[]{:S(2)}) copy-start(f32[96,64]{0,1:T(8,128)S(1)} %copy.456) | copy-start | bytes 73732
  85.4 30.0 %copy-start.4 = (f32[192,128]{0,1:T(8,128)}, f32[192,128]{0,1:T(8,128)S(1)}, u32[]{:S(2)}) copy-start(f32[192,128]{0,1:T(8,128)S(1)} %copy.448) | copy-start | bytes 294916
  85.4 25.4 %copy-start.21 = (f32[48,32]{0,1:T(8,128)S(1)}, f32[48,32]{0,1:T(8,128)}, u32[]{:S(2)}) copy-start(f32[48,32]{0,1:T(8,128)} %slice_reduce_fusion.5) | copy-start | bytes 18436
  85.4 25.4 %copy-start.24 = (f32[48,32]{0,1:T(8,128)S(1)}, f32[48,32]{0,1:T(8,128)}, u32[]{:S(2)}) copy-start(f32[48,32]{0,1:T(8,128)} %slice_reduce_fusion.6) | copy-start | bytes 18436
  85.4 25.4 %copy-start.30 = (f32[48,32]{0,1:T(8,128)S(1)}, f32[48,32]{0,1:T(8,128)}, u32[]{:S(2)}) copy-start(f32[48,32]{0,1:T(8,128)} %copy-done.29) | copy-start | bytes 18436
  86.7 13.9 %collective-permute-start.4 = (f32[8,1,128]{1,0,2:T(8,128)S(1)}, f32[8,1,128]{1,0,2:T(8,128)S(1)}, u32[]{:S(2)}, u32[]{:S(2)}) collective-permute-start(f32[8,1,128]{1,0,2:T(8,128)S(1)} %get-tuple-element.25), channel_id=1, source_target_pairs={{0,8},{8,16},{16,24},{1,9},{9,17},{17,25},{2,10},{10,18},{18,26},{... | collective-permute-start | bytes 12296 | tf_op jit(solution)/shard_map/ppermute | solution.py:17
  90.2 15.1 %collective-permute-start.5 = (f32[8,1,128]{1,0,2:T(8,128)S(1)}, f32[8,1,128]{1,0,2:T(8,128)S(1)}, u32[]{:S(2)}, u32[]{:S(2)}) collective-permute-start(f32[8,1,128]{1,0,2:T(8,128)S(1)} %get-tuple-element.26), channel_id=1, source_target_pairs={{8,0},{16,8},{24,16},{9,1},{17,9},{25,17},{10,2},{18,10},{26,18},{... | collective-permute-start | bytes 12296 | tf_op jit(solution)/shard_map/ppermute | solution.py:20
  106.1 8.8 %collective-permute-start.6 = (f32[8,194,1]{1,0,2:T(8,128)S(1)}, f32[8,194,1]{1,0,2:T(8,128)S(1)}, u32[]{:S(2)}, u32[]{:S(2)}) collective-permute-start(f32[8,194,1]{1,0,2:T(8,128)S(1)} %get-tuple-element.23), channel_id=1, source_target_pairs={{0,1},{1,2},{2,3},{3,4},{4,5},{5,6},{6,7},{8,9},{9,10},{10,11},{11... | collective-permute-start | bytes 18632 | tf_op jit(solution)/shard_map/ppermute | solution.py:17
  109.4 6.0 %collective-permute-start.7 = (f32[8,194,1]{1,0,2:T(8,128)S(1)}, f32[8,194,1]{1,0,2:T(8,128)S(1)}, u32[]{:S(2)}, u32[]{:S(2)}) collective-permute-start(f32[8,194,1]{1,0,2:T(8,128)S(1)} %get-tuple-element.24), channel_id=1, source_target_pairs={{1,0},{2,1},{3,2},{4,3},{5,4},{6,5},{7,6},{9,8},{10,9},{11,10},{12... | collective-permute-start | bytes 18632 | tf_op jit(solution)/shard_map/ppermute | solution.py:20
  143.4 7.5 %collective-permute-start.8 = (f32[8,1,64]{1,2,0:T(8,128)S(1)}, f32[8,1,64]{1,2,0:T(8,128)S(1)}, u32[]{:S(2)}, u32[]{:S(2)}) collective-permute-start(f32[8,1,64]{1,2,0:T(8,128)S(1)} %get-tuple-element.33), channel_id=1, source_target_pairs={{0,8},{8,16},{16,24},{1,9},{9,17},{17,25},{2,10},{10,18},{18,26},{... | collective-permute-start | bytes 6152 | tf_op jit(solution)/shard_map/ppermute | solution.py:17
  146.9 8.7 %collective-permute-start.9 = (f32[8,1,64]{1,2,0:T(8,128)S(1)}, f32[8,1,64]{1,2,0:T(8,128)S(1)}, u32[]{:S(2)}, u32[]{:S(2)}) collective-permute-start(f32[8,1,64]{1,2,0:T(8,128)S(1)} %get-tuple-element.34), channel_id=1, source_target_pairs={{8,0},{16,8},{24,16},{9,1},{17,9},{25,17},{10,2},{18,10},{26,18},{... | collective-permute-start | bytes 6152 | tf_op jit(solution)/shard_map/ppermute | solution.py:20
  155.7 7.1 %collective-permute-start.10 = (f32[8,98,1]{1,2,0:T(1,128)S(1)}, f32[8,98,1]{1,2,0:T(1,128)S(1)}, u32[]{:S(2)}, u32[]{:S(2)}) collective-permute-start(f32[8,98,1]{1,2,0:T(1,128)S(1)} %get-tuple-element.27), channel_id=1, source_target_pairs={{0,1},{1,2},{2,3},{3,4},{4,5},{5,6},{6,7},{8,9},{9,10},{10,11},{11... | collective-permute-start | bytes 9416 | tf_op jit(solution)/shard_map/ppermute | solution.py:17
  159.8 6.7 %collective-permute-start.11 = (f32[8,98,1]{1,2,0:T(1,128)S(1)}, f32[8,98,1]{1,2,0:T(1,128)S(1)}, u32[]{:S(2)}, u32[]{:S(2)}) collective-permute-start(f32[8,98,1]{1,2,0:T(1,128)S(1)} %get-tuple-element.28), channel_id=1, source_target_pairs={{1,0},{2,1},{3,2},{4,3},{5,4},{6,5},{7,6},{9,8},{10,9},{11,10},{12... | collective-permute-start | bytes 9416 | tf_op jit(solution)/shard_map/ppermute | solution.py:20
  177.9 5.5 collective-permute-start.12
  180.1 7.1 %collective-permute-start.13 = (f32[8,1,32]{1,2,0:T(8,128)S(1)}, f32[8,1,32]{1,2,0:T(8,128)S(1)}, u32[]{:S(2)}, u32[]{:S(2)}) collective-permute-start(f32[8,1,32]{1,2,0:T(8,128)S(1)} %get-tuple-element.95), channel_id=1, source_target_pairs={{8,0},{16,8},{24,16},{9,1},{17,9},{25,17},{10,2},{18,10},{26,18},{... | collective-permute-start | bytes 3080 | tf_op jit(solution)/shard_map/ppermute | solution.py:20
  187.4 5.7 %collective-permute-start.14 = (f32[8,50,1]{1,2,0:T(1,128)S(1)}, f32[8,50,1]{1,2,0:T(1,128)S(1)}, u32[]{:S(2)}, u32[]{:S(2)}) collective-permute-start(f32[8,50,1]{1,2,0:T(1,128)S(1)} %get-tuple-element.31), channel_id=1, source_target_pairs={{0,1},{1,2},{2,3},{3,4},{4,5},{5,6},{6,7},{8,9},{9,10},{10,11},{11... | collective-permute-start | bytes 4808 | tf_op jit(solution)/shard_map/ppermute | solution.py:17
  190.2 5.3 collective-permute-start.15
  197.7 6.4 %collective-permute-start.16 = (f32[13,24,16]{0,2,1:T(8,128)S(1)}, f32[13,24,16]{0,2,1:T(8,128)S(1)}, u32[]{:S(2)}, u32[]{:S(2)}) collective-permute-start(f32[13,24,16]{0,2,1:T(8,128)S(1)} %concatenate.161), channel_id=1, source_target_pairs={{0,8},{8,0},{16,24},{24,16},{1,9},{9,1},{17,25},{25,17},{2,10},{10... | collective-permute-start | bytes 59912 | tf_op jit(solution)/shard_map/ppermute | solution.py:32
  204.4 2.2 collective-permute-start.17
  207.0 11.3 %collective-permute-start.18 = (f32[8,1,32]{1,2,0:T(8,128)S(1)}, f32[8,1,32]{1,2,0:T(8,128)S(1)}, u32[]{:S(2)}, u32[]{:S(2)}) collective-permute-start(f32[8,1,32]{1,2,0:T(8,128)S(1)} %get-tuple-element.93), channel_id=1, source_target_pairs={{0,16},{8,24},{1,17},{9,25},{2,18},{10,26},{3,19},{11,27},{4,20},{... | collective-permute-start | bytes 3080 | tf_op jit(solution)/shard_map/ppermute | solution.py:28
  208.4 11.0 %collective-permute-start.19 = (f32[8,1,32]{1,2,0:T(8,128)S(1)}, f32[8,1,32]{1,2,0:T(8,128)S(1)}, u32[]{:S(2)}, u32[]{:S(2)}) collective-permute-start(f32[8,1,32]{1,2,0:T(8,128)S(1)} %get-tuple-element.92), channel_id=1, source_target_pairs={{16,0},{24,8},{17,1},{25,9},{18,2},{26,10},{19,3},{27,11},{20,4},{... | collective-permute-start | bytes 3080 | tf_op jit(solution)/shard_map/ppermute | solution.py:28
  209.7 9.7 %collective-permute-start.20 = (f32[8,48,1]{1,2,0:T(1,128)S(1)}, f32[8,48,1]{1,2,0:T(1,128)S(1)}, u32[]{:S(2)}, u32[]{:S(2)}) collective-permute-start(f32[8,48,1]{1,2,0:T(1,128)S(1)} %get-tuple-element.89), channel_id=1, source_target_pairs={{0,2},{1,3},{2,4},{3,5},{4,6},{5,7},{8,10},{9,11},{10,12},{11,13},... | collective-permute-start | bytes 4616 | tf_op jit(solution)/shard_map/ppermute | solution.py:28
  214.2 5.5 collective-permute-start.21
  221.6 11.2 %collective-permute-start.22 = (f32[13,24,16]{0,2,1:T(8,128)S(1)}, f32[13,24,16]{0,2,1:T(8,128)S(1)}, u32[]{:S(2)}, u32[]{:S(2)}) collective-permute-start(f32[13,24,16]{0,2,1:T(8,128)S(1)} %concatenate.170), channel_id=1, source_target_pairs={{0,16},{8,24},{16,0},{24,8},{1,17},{9,25},{17,1},{25,9},{2,18},{10... | collective-permute-start | bytes 59912 | tf_op jit(solution)/shard_map/ppermute | solution.py:32
  233.1 5.4 collective-permute-start.23
  238.8 6.0 %collective-permute-start.24 = (f32[8,1,32]{1,2,0:T(8,128)S(1)}, f32[8,1,32]{1,2,0:T(8,128)S(1)}, u32[]{:S(2)}, u32[]{:S(2)}) collective-permute-start(f32[8,1,32]{1,2,0:T(8,128)S(1)} %get-tuple-element.40), channel_id=1, source_target_pairs={} | collective-permute-start | bytes 3080 | tf_op jit(solution)/shard_map/ppermute | solution.py:28
  239.5 5.4 collective-permute-start.25
  240.1 4.7 collective-permute-start.26
  243.5 5.5 collective-permute-start.27
  327.9 6.8 %collective-permute-start.28 = (f32[8,1,32]{1,2,0:T(8,128)S(1)}, f32[8,1,32]{1,2,0:T(8,128)S(1)}, u32[]{:S(2)}, u32[]{:S(2)}) collective-permute-start(f32[8,1,32]{1,2,0:T(8,128)S(1)} %get-tuple-element.78), channel_id=1, source_target_pairs={} | collective-permute-start | bytes 3080 | tf_op jit(solution)/shard_map/ppermute | solution.py:28
  328.5 6.2 %collective-permute-start.29 = (f32[8,1,32]{1,2,0:T(8,128)S(1)}, f32[8,1,32]{1,2,0:T(8,128)S(1)}, u32[]{:S(2)}, u32[]{:S(2)}) collective-permute-start(f32[8,1,32]{1,2,0:T(8,128)S(1)} %get-tuple-element.79), channel_id=1, source_target_pairs={} | collective-permute-start | bytes 3080 | tf_op jit(solution)/shard_map/ppermute | solution.py:28
  329.2 5.5 collective-permute-start.30
  333.4 5.5 collective-permute-start.31
  419.2 6.8 %collective-permute-start.32 = (f32[8,1,32]{1,2,0:T(8,128)S(1)}, f32[8,1,32]{1,2,0:T(8,128)S(1)}, u32[]{:S(2)}, u32[]{:S(2)}) collective-permute-start(f32[8,1,32]{1,2,0:T(8,128)S(1)} %get-tuple-element.70), channel_id=1, source_target_pairs={} | collective-permute-start | bytes 3080 | tf_op jit(solution)/shard_map/ppermute | solution.py:28
  419.9 6.2 %collective-permute-start.33 = (f32[8,1,32]{1,2,0:T(8,128)S(1)}, f32[8,1,32]{1,2,0:T(8,128)S(1)}, u32[]{:S(2)}, u32[]{:S(2)}) collective-permute-start(f32[8,1,32]{1,2,0:T(8,128)S(1)} %get-tuple-element.71), channel_id=1, source_target_pairs={} | collective-permute-start | bytes 3080 | tf_op jit(solution)/shard_map/ppermute | solution.py:28
  420.5 5.5 collective-permute-start.34
  424.7 5.5 collective-permute-start.35
  509.1 6.9 %collective-permute-start.36 = (f32[8,1,32]{1,2,0:T(8,128)S(1)}, f32[8,1,32]{1,2,0:T(8,128)S(1)}, u32[]{:S(2)}, u32[]{:S(2)}) collective-permute-start(f32[8,1,32]{1,2,0:T(8,128)S(1)} %get-tuple-element.69), channel_id=1, source_target_pairs={} | collective-permute-start | bytes 3080 | tf_op jit(solution)/shard_map/ppermute | solution.py:28
  509.7 6.3 %collective-permute-start.37 = (f32[8,1,32]{1,2,0:T(8,128)S(1)}, f32[8,1,32]{1,2,0:T(8,128)S(1)}, u32[]{:S(2)}, u32[]{:S(2)}) collective-permute-start(f32[8,1,32]{1,2,0:T(8,128)S(1)} %get-tuple-element.68), channel_id=1, source_target_pairs={} | collective-permute-start | bytes 3080 | tf_op jit(solution)/shard_map/ppermute | solution.py:28
  510.4 5.6 collective-permute-start.38
  514.6 5.5 collective-permute-start.39
  (25 other events, 306.2 us)
where the time goes:
time: 573 us; the launch traced here: 563 us
  blocking collectives  274 us (48%)
  starting transfers between devices  78.8 us (14%)
  local copies, waits for them, and re-layouts  78.5 us (14%)
  waiting for transfers between devices  67.8 us (12%)
  other arithmetic  62.1 us (11%)
    psum x4, blocking collectives, norm_sum(): return lax.psum(local_dot(values, values), ('row', 'col'))  160 us
    psum x3, blocking collectives, coarse_solve(): step_size = norm_now / lax.psum(local_dot(direction, image), ('row', 'col'))  113 us
    ppermute x20, starting transfers between devices, shifted(): return lax.ppermute(block, axis, route)  35.1 us
    ppermute x8, starting transfers between devices, padded_2(): lax.ppermute(lax.slice_in_dim(block, block.shape[dim] - width, None, axis...  25.6 us
    ppermute x8, waiting for transfers between devices, padded_2(): lax.ppermute(lax.slice_in_dim(block, 0, width, axis=dim), axis, backward)  23 us
    reduce_sum x4, other arithmetic, restrict_field(): values.reshape(count, rows_here // 2, 2, cols_here // 2, 2).sum(axis=(2, 4))  19.1 us
    ppermute x20, waiting for transfers between devices, shifted(): return lax.ppermute(block, axis, route)  17.9 us
    ppermute x4, waiting for transfers between devices, partner_2(): lax.ppermute(shard, axis, [(i, i ^ 1 << apart) for i in range(lax.axis_si...  17.4 us
  transfers between devices with their start and end apart: 40, of which 19 were waited for; matrix products, arithmetic and copies ran while one was open for 6% of the time, Pallas kernels for 0%

commit v1 on v0

--- a/solution.py
+++ b/solution.py
@@ -1,3 +1,4 @@
+import functools
 from functools import partial
 import jax
 import jax.numpy as jnp
@@ -7,6 +8,13 @@
 RHS = 8
 ITERS = 4
 OMEGA = 0.8
+
+
+def trees_treat(w_in, mesh_dim, axis_tag):
+    return jax.lax.psum(jax.lax.psum(w_in, mesh_dim), axis_tag)
+
+
+see_roads = functools.partial(trees_treat, mesh_dim="col", axis_tag="row")
 
 
 def padded_2(block, sides, width):
@@ -155,7 +163,7 @@
     norm_now = norm_sum(residual)
     for sweep in range(ITERS):
         image = apply_operator(direction, coeffs, sides_of(direction))
-        step_size = norm_now / lax.psum(local_dot(direction, image), ("row", "col"))
+        step_size = norm_now / see_roads(local_dot(direction, image))
         solution = solution + expand(step_size) * direction
         if sweep + 1 < ITERS:
             residual = residual - expand(step_size) * image

time: 573 us -> 541 us (0.944)
  blocking collectives: 274 us -> 242 us
    psum x3 -> x8, blocking collectives: 113 us -> 88.2 us  [trees_treat(): return jax.lax.psum(jax.lax.psum(w_in, mesh_dim), axis_tag)]
    psum x4, blocking collectives: 160 us -> 154 us  [norm_sum(): return lax.psum(local_dot(values, values), ('row', 'col'))]
where the time goes in v1:
time: 541 us; the launch traced here: 531 us
  blocking collectives  242 us (45%)
  local copies, waits for them, and re-layouts  78.9 us (15%)
  starting transfers between devices  78.7 us (15%)
  waiting for transfers between devices  67.9 us (13%)
  other arithmetic  62.1 us (11%)
    psum x4, blocking collectives, norm_sum(): return lax.psum(local_dot(values, values), ('row', 'col'))  154 us
    psum x8, blocking collectives, trees_treat(): return jax.lax.psum(jax.lax.psum(w_in, mesh_dim), axis_tag)  88.2 us
    ppermute x20, starting transfers between devices, shifted(): return lax.ppermute(block, axis, route)  35 us
    ppermute x8, starting transfers between devices, padded_2(): lax.ppermute(lax.slice_in_dim(block, block.shape[dim] - width, None, axis...  25.6 us
    ppermute x8, waiting for transfers between devices, padded_2(): lax.ppermute(lax.slice_in_dim(block, 0, width, axis=dim), axis, backward)  23 us
    reduce_sum x4, other arithmetic, restrict_field(): values.reshape(count, rows_here // 2, 2, cols_here // 2, 2).sum(axis=(2, 4))  19.1 us
    ppermute x20, waiting for transfers between devices, shifted(): return lax.ppermute(block, axis, route)  17.9 us
    ppermute x4, waiting for transfers between devices, partner_2(): lax.ppermute(shard, axis, [(i, i ^ 1 << apart) for i in range(lax.axis_si...  17.4 us
  transfers between devices with their start and end apart: 40, of which 19 were waited for; matrix products, arithmetic and copies ran while one was open for 6% of the time, Pallas kernels for 0%

profile of v1, /device:TPU:0, one launch (start us, length us, event | category | flops | bytes accessed | tf_op | source)
XLA Modules:
  0.0 531.5 jit_solution(14172915156742882052)
XLA Ops:
  1.6 4.9 collective-permute-start
  8.8 3.2 collective-permute-done.1
  17.3 8.4 %squeeze.46 = f32[96,2,64,2]{3,2,1,0:T(8,128)} reshape(f32[192,128]{1,0:T(8,128)} %param.5) | data formatting | bytes 196608 | tf_op jit(solution)/shard_map/squeeze | solution.py:80
  25.6 3.7 reduce_sum.289
  34.1 7.6 %squeeze.47 = f32[96,2,64,2]{3,2,1,0:T(8,128)} reshape(f32[192,128]{1,0:T(8,128)S(1)} %get-tuple-element.17) | data formatting | bytes 196608 | tf_op jit(solution)/shard_map/squeeze | solution.py:81
  41.6 7.6 %squeeze.48 = f32[96,2,64,2]{3,2,1,0:T(8,128)} reshape(f32[192,128]{1,0:T(8,128)S(1)} %get-tuple-element.18) | data formatting | bytes 196608 | tf_op jit(solution)/shard_map/squeeze | solution.py:82
  49.2 4.6 slice_reduce_fusion.2
  54.0 7.6 %squeeze.49 = f32[96,2,64,2]{3,2,1,0:T(8,128)} reshape(f32[192,128]{1,0:T(8,128)S(1)} %get-tuple-element.19) | data formatting | bytes 196608 | tf_op jit(solution)/shard_map/squeeze | solution.py:83
  61.6 8.1 %squeeze.50 = f32[96,2,64,2]{3,2,1,0:T(8,128)} reshape(f32[192,128]{1,0:T(8,128)S(1)} %get-tuple-element.20) | data formatting | bytes 196608 | tf_op jit(solution)/shard_map/squeeze | solution.py:84
  69.7 7.9 %slice_reduce_fusion = (f32[96,64]{1,0:T(8,128)S(1)}, f32[96,64]{1,0:T(8,128)S(1)}) fusion(f32[96,2,64,2]{3,2,1,0:T(8,128)} %squeeze.50, f32[96,2,64,2]{3,2,1,0:T(8,128)} %squeeze.49), kind=kLoop, calls=%fused_computation | loop fusion | flops 12288 | bytes 147456 | tf_op jit(solution)/shard_map/reduce_sum | solution.py:84
  87.1 3.5 collective-permute-start.4
  92.2 8.8 %collective-permute-done.4 = f32[8,1,128]{1,0,2:T(8,128)S(1)} collective-permute-done((f32[8,1,128]{1,0,2:T(8,128)S(1)}, f32[8,1,128]{1,0,2:T(8,128)S(1)}, u32[]{:S(2)}, u32[]{:S(2)}) %collective-permute-start.4) | collective-permute-done | bytes 4128 | tf_op jit(solution)/shard_map/ppermute | solution.py:25
  101.0 4.7 collective-permute-done.5
  106.5 3.3 collective-permute-start.6
  115.8 4.1 fusion.3
  119.9 7.0 %copy.453 = f32[8,192,128]{0,2,1:T(8,128)} copy(f32[8,192,128]{1,0,2:T(8,128)S(1)} %fusion.3) | data formatting | bytes 1572864 | tf_op jit(solution)/shard_map/sub | solution.py:111
  126.9 14.0 %reduce_sum.288 = f32[8,96,64]{0,2,1:T(8,128)S(1)} reduce(f32[8,96,2,64,2]{0,4,3,2,1:T(2,128)} %bitcast.80, f32[]{:T(128)} %constant.67.clone.1), dimensions={2,4}, to_apply=%region_0.0 | reduce | flops 147456 | bytes 983044 | tf_op jit(solution)/shard_map/reduce_sum | solution.py:74
  143.8 3.5 collective-permute-start.8
  151.3 4.7 collective-permute-done.9
  156.1 4.1 collective-permute-start.10
  163.2 3.6 collective-permute-done.11
  168.1 3.7 copy.461
  171.9 3.9 reduce_sum.294
  183.8 3.9 collective-permute-done.13
  198.6 5.9 %collective-permute-done.16 = f32[13,24,16]{0,2,1:T(8,128)S(1)} collective-permute-done((f32[13,24,16]{0,2,1:T(8,128)S(1)}, f32[13,24,16]{0,2,1:T(8,128)S(1)}, u32[]{:S(2)}, u32[]{:S(2)}) %collective-permute-start.16) | collective-permute-done | bytes 20000 | tf_op jit(solution)/shard_map/ppermute | solution.py:40
  210.0 4.5 collective-permute-start.20
  221.9 3.6 collective-permute-start.22
  225.7 7.4 %collective-permute-done.22 = f32[13,24,16]{0,2,1:T(8,128)S(1)} collective-permute-done((f32[13,24,16]{0,2,1:T(8,128)S(1)}, f32[13,24,16]{0,2,1:T(8,128)S(1)}, u32[]{:S(2)}, u32[]{:S(2)}) %collective-permute-start.22) | collective-permute-done | bytes 20000 | tf_op jit(solution)/shard_map/ppermute | solution.py:40
  240.5 3.4 collective-permute-start.26
  245.2 4.2 collective-permute-done.27
  249.6 11.8 %psum.85 = f32[8]{0:T(128)S(1)} all-reduce(f32[8]{0:T(128)S(1)} %broadcast_multiply_fusion.6), channel_id=1, replica_groups=mesh['row'=4,'col'=8] {'col'}, use_global_device_ids=true, to_apply=%region_27.28 | all-reduce | flops 8 | bytes 64 | tf_op jit(solution)/shard_map/psum | solution.py:14
  261.4 10.8 %psum.86 = f32[8]{0:T(128)S(1)} all-reduce(f32[8]{0:T(128)S(1)} %psum.85), channel_id=1, replica_groups=mesh['row'=4,'col'=8] {'row'}, use_global_device_ids=true, to_apply=%region_28.29 | all-reduce | flops 8 | bytes 64 | tf_op jit(solution)/shard_map/psum | solution.py:14
  272.2 37.2 %psum.84 = f32[8]{0:T(128)S(1)} all-reduce(f32[8]{0:T(128)S(1)} %broadcast_multiply_fusion.7), channel_id=1, replica_groups=mesh['row'=4,'col'=8] {'row','col'}, use_global_device_ids=true, to_apply=%region_25.26 | all-reduce | flops 8 | bytes 64 | tf_op jit(solution)/shard_map/psum | solution.py:155
  309.6 40.6 %psum.87 = f32[8]{0:T(128)S(1)} all-reduce(f32[8]{0:T(128)S(1)} %broadcast_multiply_fusion.5), channel_id=1, replica_groups=mesh['row'=4,'col'=8] {'row','col'}, use_global_device_ids=true, to_apply=%region_30.31 | all-reduce | flops 8 | bytes 64 | tf_op jit(solution)/shard_map/psum | solution.py:155
  351.9 4.2 collective-permute-start.30
  357.4 4.1 collective-permute-done.31
  361.8 11.8 %psum.88 = f32[8]{0:T(128)S(1)} all-reduce(f32[8]{0:T(128)S(1)} %broadcast_multiply_fusion.4), channel_id=1, replica_groups=mesh['row'=4,'col'=8] {'col'}, use_global_device_ids=true, to_apply=%region_32.33 | all-reduce | flops 8 | bytes 64 | tf_op jit(solution)/shard_map/psum | solution.py:14
  373.6 9.9 %psum.89 = f32[8]{0:T(128)S(1)} all-reduce(f32[8]{0:T(128)S(1)} %psum.88), channel_id=1, replica_groups=mesh['row'=4,'col'=8] {'row'}, use_global_device_ids=true, to_apply=%region_33.34 | all-reduce | flops 8 | bytes 64 | tf_op jit(solution)/shard_map/psum | solution.py:14
  383.8 38.1 %psum.90 = f32[8]{0:T(128)S(1)} all-reduce(f32[8]{0:T(128)S(1)} %broadcast_multiply_fusion.3), channel_id=1, replica_groups=mesh['row'=4,'col'=8] {'row','col'}, use_global_device_ids=true, to_apply=%region_35.36 | all-reduce | flops 8 | bytes 64 | tf_op jit(solution)/shard_map/psum | solution.py:155
  423.5 4.2 collective-permute-start.34
  429.0 4.1 collective-permute-done.35
  433.4 11.8 %psum.91 = f32[8]{0:T(128)S(1)} all-reduce(f32[8]{0:T(128)S(1)} %broadcast_multiply_fusion.2), channel_id=1, replica_groups=mesh['row'=4,'col'=8] {'col'}, use_global_device_ids=true, to_apply=%region_37.38 | all-reduce | flops 8 | bytes 64 | tf_op jit(solution)/shard_map/psum | solution.py:14
  445.2 10.0 %psum.92 = f32[8]{0:T(128)S(1)} all-reduce(f32[8]{0:T(128)S(1)} %psum.91), channel_id=1, replica_groups=mesh['row'=4,'col'=8] {'row'}, use_global_device_ids=true, to_apply=%region_38.39 | all-reduce | flops 8 | bytes 64 | tf_op jit(solution)/shard_map/psum | solution.py:14
  455.5 38.0 %psum.93 = f32[8]{0:T(128)S(1)} all-reduce(f32[8]{0:T(128)S(1)} %broadcast_multiply_fusion.1), channel_id=1, replica_groups=mesh['row'=4,'col'=8] {'row','col'}, use_global_device_ids=true, to_apply=%region_40.41 | all-reduce | flops 8 | bytes 64 | tf_op jit(solution)/shard_map/psum | solution.py:155
  495.1 4.2 collective-permute-start.38
  500.7 4.1 collective-permute-done.39
  505.0 11.8 %psum.94 = f32[8]{0:T(128)S(1)} all-reduce(f32[8]{0:T(128)S(1)} %broadcast_multiply_fusion), channel_id=1, replica_groups=mesh['row'=4,'col'=8] {'col'}, use_global_device_ids=true, to_apply=%region_42.43 | all-reduce | flops 8 | bytes 64 | tf_op jit(solution)/shard_map/psum | solution.py:14
  516.8 10.3 %psum.95 = f32[8]{0:T(128)S(1)} all-reduce(f32[8]{0:T(128)S(1)} %psum.94), channel_id=1, replica_groups=mesh['row'=4,'col'=8] {'row'}, use_global_device_ids=true, to_apply=%region_43.44 | all-reduce | flops 8 | bytes 64 | tf_op jit(solution)/shard_map/psum | solution.py:14
  (287 shorter events, 97.3 us)
Async XLA Ops:
  1.6 7.2 %collective-permute-start = (f32[2,1,128]{2,1,0:T(1,128)S(1)}, f32[2,1,128]{2,1,0:T(1,128)S(1)}, u32[]{:S(2)}, u32[]{:S(2)}) collective-permute-start(f32[2,1,128]{2,1,0:T(1,128)S(1)} %get-tuple-element.58), channel_id=1, source_target_pairs={{0,8},{8,16},{16,24},{1,9},{9,17},{17,25},{2,10},{10,18},{18,26},{... | collective-permute-start | bytes 3080 | tf_op jit(solution)/shard_map/ppermute | solution.py:25
  6.6 5.5 %collective-permute-start.1 = (f32[2,1,128]{2,1,0:T(1,128)S(1)}, f32[2,1,128]{2,1,0:T(1,128)S(1)}, u32[]{:S(2)}, u32[]{:S(2)}) collective-permute-start(f32[2,1,128]{2,1,0:T(1,128)S(1)} %get-tuple-element.59), channel_id=1, source_target_pairs={{8,0},{16,8},{24,16},{9,1},{17,9},{25,17},{10,2},{18,10},{26,18},{... | collective-permute-start | bytes 3080 | tf_op jit(solution)/shard_map/ppermute | solution.py:28
  13.1 18.8 %collective-permute-start.2 = (f32[2,194,1]{2,1,0:T(8,128)S(1)}, f32[2,194,1]{2,1,0:T(8,128)S(1)}, u32[]{:S(2)}, u32[]{:S(2)}) collective-permute-start(f32[2,194,1]{2,1,0:T(8,128)S(1)} %get-tuple-element.56), channel_id=1, source_target_pairs={{0,1},{1,2},{2,3},{3,4},{4,5},{5,6},{6,7},{8,9},{9,10},{10,11},{11... | collective-permute-start | bytes 4664 | tf_op jit(solution)/shard_map/ppermute | solution.py:25
  14.4 17.5 %collective-permute-start.3 = (f32[2,194,1]{2,1,0:T(8,128)S(1)}, f32[2,194,1]{2,1,0:T(8,128)}, u32[]{:S(2)}, u32[]{:S(2)}) collective-permute-start(f32[2,194,1]{2,1,0:T(8,128)S(1)} %get-tuple-element.57), channel_id=1, source_target_pairs={{1,0},{2,1},{3,2},{4,3},{5,4},{6,5},{7,6},{9,8},{10,9},{11,10},{12... | collective-permute-start | bytes 4664 | tf_op jit(solution)/shard_map/ppermute | solution.py:28
  30.6 85.1 %copy-start = (f32[192,128]{0,1:T(8,128)}, f32[192,128]{0,1:T(8,128)S(1)}, u32[]{:S(2)}) copy-start(f32[192,128]{0,1:T(8,128)S(1)} %copy.445) | copy-start | bytes 294916
  30.7 85.0 %copy-start.2 = (f32[192,128]{0,1:T(8,128)}, f32[192,128]{0,1:T(8,128)S(1)}, u32[]{:S(2)}) copy-start(f32[192,128]{0,1:T(8,128)S(1)} %copy.447) | copy-start | bytes 294916
  53.9 25.2 %copy-start.13 = (f32[96,64]{0,1:T(8,128)}, f32[96,64]{0,1:T(8,128)S(1)}, u32[]{:S(2)}) copy-start(f32[96,64]{0,1:T(8,128)S(1)} %copy.457) | copy-start | bytes 73732
  54.0 26.6 %copy-start.15 = (f32[96,64]{0,1:T(8,128)}, f32[96,64]{0,1:T(8,128)S(1)}, u32[]{:S(2)}) copy-start(f32[96,64]{0,1:T(8,128)S(1)} %copy.456) | copy-start | bytes 73732
  85.7 30.0 %copy-start.4 = (f32[192,128]{0,1:T(8,128)}, f32[192,128]{0,1:T(8,128)S(1)}, u32[]{:S(2)}) copy-start(f32[192,128]{0,1:T(8,128)S(1)} %copy.448) | copy-start | bytes 294916
  85.8 25.4 %copy-start.21 = (f32[48,32]{0,1:T(8,128)S(1)}, f32[48,32]{0,1:T(8,128)}, u32[]{:S(2)}) copy-start(f32[48,32]{0,1:T(8,128)} %slice_reduce_fusion.5) | copy-start | bytes 18436
  85.8 25.4 %copy-start.24 = (f32[48,32]{0,1:T(8,128)S(1)}, f32[48,32]{0,1:T(8,128)}, u32[]{:S(2)}) copy-start(f32[48,32]{0,1:T(8,128)} %slice_reduce_fusion.6) | copy-start | bytes 18436
  85.8 25.4 %copy-start.30 = (f32[48,32]{0,1:T(8,128)S(1)}, f32[48,32]{0,1:T(8,128)}, u32[]{:S(2)}) copy-start(f32[48,32]{0,1:T(8,128)} %copy-done.29) | copy-start | bytes 18436
  87.1 13.9 %collective-permute-start.4 = (f32[8,1,128]{1,0,2:T(8,128)S(1)}, f32[8,1,128]{1,0,2:T(8,128)S(1)}, u32[]{:S(2)}, u32[]{:S(2)}) collective-permute-start(f32[8,1,128]{1,0,2:T(8,128)S(1)} %get-tuple-element.23), channel_id=1, source_target_pairs={{0,8},{8,16},{16,24},{1,9},{9,17},{17,25},{2,10},{10,18},{18,26},{... | collective-permute-start | bytes 12296 | tf_op jit(solution)/shard_map/ppermute | solution.py:25
  90.6 15.1 %collective-permute-start.5 = (f32[8,1,128]{1,0,2:T(8,128)S(1)}, f32[8,1,128]{1,0,2:T(8,128)S(1)}, u32[]{:S(2)}, u32[]{:S(2)}) collective-permute-start(f32[8,1,128]{1,0,2:T(8,128)S(1)} %get-tuple-element.24), channel_id=1, source_target_pairs={{8,0},{16,8},{24,16},{9,1},{17,9},{25,17},{10,2},{18,10},{26,18},{... | collective-permute-start | bytes 12296 | tf_op jit(solution)/shard_map/ppermute | solution.py:28
  106.5 8.8 %collective-permute-start.6 = (f32[8,194,1]{1,0,2:T(8,128)S(1)}, f32[8,194,1]{1,0,2:T(8,128)S(1)}, u32[]{:S(2)}, u32[]{:S(2)}) collective-permute-start(f32[8,194,1]{1,0,2:T(8,128)S(1)} %get-tuple-element.21), channel_id=1, source_target_pairs={{0,1},{1,2},{2,3},{3,4},{4,5},{5,6},{6,7},{8,9},{9,10},{10,11},{11... | collective-permute-start | bytes 18632 | tf_op jit(solution)/shard_map/ppermute | solution.py:25
  109.8 6.0 %collective-permute-start.7 = (f32[8,194,1]{1,0,2:T(8,128)S(1)}, f32[8,194,1]{1,0,2:T(8,128)S(1)}, u32[]{:S(2)}, u32[]{:S(2)}) collective-permute-start(f32[8,194,1]{1,0,2:T(8,128)S(1)} %get-tuple-element.22), channel_id=1, source_target_pairs={{1,0},{2,1},{3,2},{4,3},{5,4},{6,5},{7,6},{9,8},{10,9},{11,10},{12... | collective-permute-start | bytes 18632 | tf_op jit(solution)/shard_map/ppermute | solution.py:28
  143.8 7.5 %collective-permute-start.8 = (f32[8,1,64]{1,2,0:T(8,128)S(1)}, f32[8,1,64]{1,2,0:T(8,128)S(1)}, u32[]{:S(2)}, u32[]{:S(2)}) collective-permute-start(f32[8,1,64]{1,2,0:T(8,128)S(1)} %get-tuple-element.31), channel_id=1, source_target_pairs={{0,8},{8,16},{16,24},{1,9},{9,17},{17,25},{2,10},{10,18},{18,26},{... | collective-permute-start | bytes 6152 | tf_op jit(solution)/shard_map/ppermute | solution.py:25
  147.2 8.7 %collective-permute-start.9 = (f32[8,1,64]{1,2,0:T(8,128)S(1)}, f32[8,1,64]{1,2,0:T(8,128)S(1)}, u32[]{:S(2)}, u32[]{:S(2)}) collective-permute-start(f32[8,1,64]{1,2,0:T(8,128)S(1)} %get-tuple-element.32), channel_id=1, source_target_pairs={{8,0},{16,8},{24,16},{9,1},{17,9},{25,17},{10,2},{18,10},{26,18},{... | collective-permute-start | bytes 6152 | tf_op jit(solution)/shard_map/ppermute | solution.py:28
  156.1 7.1 %collective-permute-start.10 = (f32[8,98,1]{1,2,0:T(1,128)S(1)}, f32[8,98,1]{1,2,0:T(1,128)S(1)}, u32[]{:S(2)}, u32[]{:S(2)}) collective-permute-start(f32[8,98,1]{1,2,0:T(1,128)S(1)} %get-tuple-element.25), channel_id=1, source_target_pairs={{0,1},{1,2},{2,3},{3,4},{4,5},{5,6},{6,7},{8,9},{9,10},{10,11},{11... | collective-permute-start | bytes 9416 | tf_op jit(solution)/shard_map/ppermute | solution.py:25
  160.2 6.7 %collective-permute-start.11 = (f32[8,98,1]{1,2,0:T(1,128)S(1)}, f32[8,98,1]{1,2,0:T(1,128)S(1)}, u32[]{:S(2)}, u32[]{:S(2)}) collective-permute-start(f32[8,98,1]{1,2,0:T(1,128)S(1)} %get-tuple-element.26), channel_id=1, source_target_pairs={{1,0},{2,1},{3,2},{4,3},{5,4},{6,5},{7,6},{9,8},{10,9},{11,10},{12... | collective-permute-start | bytes 9416 | tf_op jit(solution)/shard_map/ppermute | solution.py:28
  178.3 5.5 %collective-permute-start.12 = (f32[8,1,32]{1,2,0:T(8,128)S(1)}, f32[8,1,32]{1,2,0:T(8,128)S(1)}, u32[]{:S(2)}, u32[]{:S(2)}) collective-permute-start(f32[8,1,32]{1,2,0:T(8,128)S(1)} %get-tuple-element.92), channel_id=1, source_target_pairs={{0,8},{8,16},{16,24},{1,9},{9,17},{17,25},{2,10},{10,18},{18,26},{... | collective-permute-start | bytes 3080 | tf_op jit(solution)/shard_map/ppermute | solution.py:25
  180.5 7.1 %collective-permute-start.13 = (f32[8,1,32]{1,2,0:T(8,128)S(1)}, f32[8,1,32]{1,2,0:T(8,128)S(1)}, u32[]{:S(2)}, u32[]{:S(2)}) collective-permute-start(f32[8,1,32]{1,2,0:T(8,128)S(1)} %get-tuple-element.93), channel_id=1, source_target_pairs={{8,0},{16,8},{24,16},{9,1},{17,9},{25,17},{10,2},{18,10},{26,18},{... | collective-permute-start | bytes 3080 | tf_op jit(solution)/shard_map/ppermute | solution.py:28
  187.7 5.7 %collective-permute-start.14 = (f32[8,50,1]{1,2,0:T(1,128)S(1)}, f32[8,50,1]{1,2,0:T(1,128)S(1)}, u32[]{:S(2)}, u32[]{:S(2)}) collective-permute-start(f32[8,50,1]{1,2,0:T(1,128)S(1)} %get-tuple-element.29), channel_id=1, source_target_pairs={{0,1},{1,2},{2,3},{3,4},{4,5},{5,6},{6,7},{8,9},{9,10},{10,11},{11... | collective-permute-start | bytes 4808 | tf_op jit(solution)/shard_map/ppermute | solution.py:25
  190.6 5.3 %collective-permute-start.15 = (f32[8,50,1]{1,2,0:T(1,128)S(1)}, f32[8,50,1]{1,2,0:T(1,128)S(1)}, u32[]{:S(2)}, u32[]{:S(2)}) collective-permute-start(f32[8,50,1]{1,2,0:T(1,128)S(1)} %get-tuple-element.30), channel_id=1, source_target_pairs={{1,0},{2,1},{3,2},{4,3},{5,4},{6,5},{7,6},{9,8},{10,9},{11,10},{12... | collective-permute-start | bytes 4808 | tf_op jit(solution)/shard_map/ppermute | solution.py:28
  198.0 6.4 %collective-permute-start.16 = (f32[13,24,16]{0,2,1:T(8,128)S(1)}, f32[13,24,16]{0,2,1:T(8,128)S(1)}, u32[]{:S(2)}, u32[]{:S(2)}) collective-permute-start(f32[13,24,16]{0,2,1:T(8,128)S(1)} %concatenate.161), channel_id=1, source_target_pairs={{0,8},{8,0},{16,24},{24,16},{1,9},{9,1},{17,25},{25,17},{2,10},{10... | collective-permute-start | bytes 59912 | tf_op jit(solution)/shard_map/ppermute | solution.py:40
  204.8 2.2 collective-permute-start.17
  207.4 11.3 %collective-permute-start.18 = (f32[8,1,32]{1,2,0:T(8,128)S(1)}, f32[8,1,32]{1,2,0:T(8,128)S(1)}, u32[]{:S(2)}, u32[]{:S(2)}) collective-permute-start(f32[8,1,32]{1,2,0:T(8,128)S(1)} %get-tuple-element.91), channel_id=1, source_target_pairs={{0,16},{8,24},{1,17},{9,25},{2,18},{10,26},{3,19},{11,27},{4,20},{... | collective-permute-start | bytes 3080 | tf_op jit(solution)/shard_map/ppermute | solution.py:36
  208.7 11.0 %collective-permute-start.19 = (f32[8,1,32]{1,2,0:T(8,128)S(1)}, f32[8,1,32]{1,2,0:T(8,128)S(1)}, u32[]{:S(2)}, u32[]{:S(2)}) collective-permute-start(f32[8,1,32]{1,2,0:T(8,128)S(1)} %get-tuple-element.90), channel_id=1, source_target_pairs={{16,0},{24,8},{17,1},{25,9},{18,2},{26,10},{19,3},{27,11},{20,4},{... | collective-permute-start | bytes 3080 | tf_op jit(solution)/shard_map/ppermute | solution.py:36
  210.0 9.7 %collective-permute-start.20 = (f32[8,48,1]{1,2,0:T(1,128)S(1)}, f32[8,48,1]{1,2,0:T(1,128)S(1)}, u32[]{:S(2)}, u32[]{:S(2)}) collective-permute-start(f32[8,48,1]{1,2,0:T(1,128)S(1)} %get-tuple-element.87), channel_id=1, source_target_pairs={{0,2},{1,3},{2,4},{3,5},{4,6},{5,7},{8,10},{9,11},{10,12},{11,13},... | collective-permute-start | bytes 4616 | tf_op jit(solution)/shard_map/ppermute | solution.py:36
  214.6 5.5 %collective-permute-start.21 = (f32[8,48,1]{1,2,0:T(1,128)S(1)}, f32[8,48,1]{1,2,0:T(1,128)S(1)}, u32[]{:S(2)}, u32[]{:S(2)}) collective-permute-start(f32[8,48,1]{1,2,0:T(1,128)S(1)} %get-tuple-element.86), channel_id=1, source_target_pairs={{2,0},{3,1},{4,2},{5,3},{6,4},{7,5},{10,8},{11,9},{12,10},{13,11},... | collective-permute-start | bytes 4616 | tf_op jit(solution)/shard_map/ppermute | solution.py:36
  221.9 11.2 %collective-permute-start.22 = (f32[13,24,16]{0,2,1:T(8,128)S(1)}, f32[13,24,16]{0,2,1:T(8,128)S(1)}, u32[]{:S(2)}, u32[]{:S(2)}) collective-permute-start(f32[13,24,16]{0,2,1:T(8,128)S(1)} %concatenate.170), channel_id=1, source_target_pairs={{0,16},{8,24},{16,0},{24,8},{1,17},{9,25},{17,1},{25,9},{2,18},{10... | collective-permute-start | bytes 59912 | tf_op jit(solution)/shard_map/ppermute | solution.py:40
  233.4 5.4 %collective-permute-start.23 = (f32[13,48,16]{1,2,0:T(8,128)S(1)}, f32[13,48,16]{1,2,0:T(8,128)S(1)}, u32[]{:S(2)}, u32[]{:S(2)}) collective-permute-start(f32[13,48,16]{1,2,0:T(8,128)S(1)} %maximum_select_fusion.3), channel_id=1, source_target_pairs={{0,2},{1,3},{2,0},{3,1},{4,6},{5,7},{6,4},{7,5},{8,10},{9,11},{10,... | collective-permute-start | bytes 119816 | tf_op jit(solution)/shard_map/ppermute | solution.py:40
  239.1 6.0 %collective-permute-start.24 = (f32[8,1,32]{1,2,0:T(8,128)S(1)}, f32[8,1,32]{1,2,0:T(8,128)S(1)}, u32[]{:S(2)}, u32[]{:S(2)}) collective-permute-start(f32[8,1,32]{1,2,0:T(8,128)S(1)} %get-tuple-element.38), channel_id=1, source_target_pairs={} | collective-permute-start | bytes 3080 | tf_op jit(solution)/shard_map/ppermute | solution.py:36
  239.8 5.4 %collective-permute-start.25 = (f32[8,1,32]{1,2,0:T(8,128)S(1)}, f32[8,1,32]{1,2,0:T(8,128)S(1)}, u32[]{:S(2)}, u32[]{:S(2)}) collective-permute-start(f32[8,1,32]{1,2,0:T(8,128)S(1)} %get-tuple-element.39), channel_id=1, source_target_pairs={} | collective-permute-start | bytes 3080 | tf_op jit(solution)/shard_map/ppermute | solution.py:36
  240.5 4.7 collective-permute-start.26
  243.8 5.5 %collective-permute-start.27 = (f32[8,48,1]{1,2,0:T(1,128)S(1)}, f32[8,48,1]{1,2,0:T(1,128)S(1)}, u32[]{:S(2)}, u32[]{:S(2)}) collective-permute-start(f32[8,48,1]{1,2,0:T(1,128)S(1)} %get-tuple-element.43), channel_id=1, source_target_pairs={{4,0},{5,1},{6,2},{7,3},{12,8},{13,9},{14,10},{15,11},{20,16},{21,... | collective-permute-start | bytes 4616 | tf_op jit(solution)/shard_map/ppermute | solution.py:36
  350.6 6.8 %collective-permute-start.28 = (f32[8,1,32]{1,2,0:T(8,128)S(1)}, f32[8,1,32]{1,2,0:T(8,128)S(1)}, u32[]{:S(2)}, u32[]{:S(2)}) collective-permute-start(f32[8,1,32]{1,2,0:T(8,128)S(1)} %get-tuple-element.76), channel_id=1, source_target_pairs={} | collective-permute-start | bytes 3080 | tf_op jit(solution)/shard_map/ppermute | solution.py:36
  351.2 6.2 %collective-permute-start.29 = (f32[8,1,32]{1,2,0:T(8,128)S(1)}, f32[8,1,32]{1,2,0:T(8,128)S(1)}, u32[]{:S(2)}, u32[]{:S(2)}) collective-permute-start(f32[8,1,32]{1,2,0:T(8,128)S(1)} %get-tuple-element.77), channel_id=1, source_target_pairs={} | collective-permute-start | bytes 3080 | tf_op jit(solution)/shard_map/ppermute | solution.py:36
  351.9 5.5 %collective-permute-start.30 = (f32[8,48,1]{1,2,0:T(1,128)S(1)}, f32[8,48,1]{1,2,0:T(1,128)S(1)}, u32[]{:S(2)}, u32[]{:S(2)}) collective-permute-start(f32[8,48,1]{1,2,0:T(1,128)S(1)} %get-tuple-element.80), channel_id=1, source_target_pairs={{0,4},{1,5},{2,6},{3,7},{8,12},{9,13},{10,14},{11,15},{16,20},{17,... | collective-permute-start | bytes 4616 | tf_op jit(solution)/shard_map/ppermute | solution.py:36
  356.1 5.5 %collective-permute-start.31 = (f32[8,48,1]{1,2,0:T(1,128)S(1)}, f32[8,48,1]{1,2,0:T(1,128)S(1)}, u32[]{:S(2)}, u32[]{:S(2)}) collective-permute-start(f32[8,48,1]{1,2,0:T(1,128)S(1)} %get-tuple-element.81), channel_id=1, source_target_pairs={{4,0},{5,1},{6,2},{7,3},{12,8},{13,9},{14,10},{15,11},{20,16},{21,... | collective-permute-start | bytes 4616 | tf_op jit(solution)/shard_map/ppermute | solution.py:36
  422.2 6.8 %collective-permute-start.32 = (f32[8,1,32]{1,2,0:T(8,128)S(1)}, f32[8,1,32]{1,2,0:T(8,128)S(1)}, u32[]{:S(2)}, u32[]{:S(2)}) collective-permute-start(f32[8,1,32]{1,2,0:T(8,128)S(1)} %get-tuple-element.68), channel_id=1, source_target_pairs={} | collective-permute-start | bytes 3080 | tf_op jit(solution)/shard_map/ppermute | solution.py:36
  422.8 6.2 %collective-permute-start.33 = (f32[8,1,32]{1,2,0:T(8,128)S(1)}, f32[8,1,32]{1,2,0:T(8,128)S(1)}, u32[]{:S(2)}, u32[]{:S(2)}) collective-permute-start(f32[8,1,32]{1,2,0:T(8,128)S(1)} %get-tuple-element.69), channel_id=1, source_target_pairs={} | collective-permute-start | bytes 3080 | tf_op jit(solution)/shard_map/ppermute | solution.py:36
  423.5 5.5 %collective-permute-start.34 = (f32[8,48,1]{1,2,0:T(1,128)S(1)}, f32[8,48,1]{1,2,0:T(1,128)S(1)}, u32[]{:S(2)}, u32[]{:S(2)}) collective-permute-start(f32[8,48,1]{1,2,0:T(1,128)S(1)} %get-tuple-element.72), channel_id=1, source_target_pairs={{0,4},{1,5},{2,6},{3,7},{8,12},{9,13},{10,14},{11,15},{16,20},{17,... | collective-permute-start | bytes 4616 | tf_op jit(solution)/shard_map/ppermute | solution.py:36
  427.7 5.5 %collective-permute-start.35 = (f32[8,48,1]{1,2,0:T(1,128)S(1)}, f32[8,48,1]{1,2,0:T(1,128)S(1)}, u32[]{:S(2)}, u32[]{:S(2)}) collective-permute-start(f32[8,48,1]{1,2,0:T(1,128)S(1)} %get-tuple-element.73), channel_id=1, source_target_pairs={{4,0},{5,1},{6,2},{7,3},{12,8},{13,9},{14,10},{15,11},{20,16},{21,... | collective-permute-start | bytes 4616 | tf_op jit(solution)/shard_map/ppermute | solution.py:36
  493.7 6.9 %collective-permute-start.36 = (f32[8,1,32]{1,2,0:T(8,128)S(1)}, f32[8,1,32]{1,2,0:T(8,128)S(1)}, u32[]{:S(2)}, u32[]{:S(2)}) collective-permute-start(f32[8,1,32]{1,2,0:T(8,128)S(1)} %get-tuple-element.67), channel_id=1, source_target_pairs={} | collective-permute-start | bytes 3080 | tf_op jit(solution)/shard_map/ppermute | solution.py:36
  494.4 6.3 %collective-permute-start.37 = (f32[8,1,32]{1,2,0:T(8,128)S(1)}, f32[8,1,32]{1,2,0:T(8,128)S(1)}, u32[]{:S(2)}, u32[]{:S(2)}) collective-permute-start(f32[8,1,32]{1,2,0:T(8,128)S(1)} %get-tuple-element.66), channel_id=1, source_target_pairs={} | collective-permute-start | bytes 3080 | tf_op jit(solution)/shard_map/ppermute | solution.py:36
  495.1 5.6 %collective-permute-start.38 = (f32[8,48,1]{1,2,0:T(1,128)S(1)}, f32[8,48,1]{1,2,0:T(1,128)S(1)}, u32[]{:S(2)}, u32[]{:S(2)}) collective-permute-start(f32[8,48,1]{1,2,0:T(1,128)S(1)} %get-tuple-element.63), channel_id=1, source_target_pairs={{0,4},{1,5},{2,6},{3,7},{8,12},{9,13},{10,14},{11,15},{16,20},{17,... | collective-permute-start | bytes 4616 | tf_op jit(solution)/shard_map/ppermute | solution.py:36
  499.2 5.5 %collective-permute-start.39 = (f32[8,48,1]{1,2,0:T(1,128)S(1)}, f32[8,48,1]{1,2,0:T(1,128)S(1)}, u32[]{:S(2)}, u32[]{:S(2)}) collective-permute-start(f32[8,48,1]{1,2,0:T(1,128)S(1)} %get-tuple-element.62), channel_id=1, source_target_pairs={{4,0},{5,1},{6,2},{7,3},{12,8},{13,9},{14,10},{15,11},{20,16},{21,... | collective-permute-start | bytes 4616 | tf_op jit(solution)/shard_map/ppermute | solution.py:36
  (25 other events, 306.2 us)
